TPU v7x, 32 devices: a whole 2x2x4 slice. The times are simulated.
32 devices in a mesh: section: 2 (over x), dp: 4 (over z), fsdp: 4 (over y, core).
Axes of the slice: x: 2, y: 2, z: 4, core: 2. Of those that a mesh axis runs over, the one named last changes fastest.
Arguments:
- inputs: float32 [32, 128, 1536], P(('dp', 'fsdp')), may hold values from -6 to 6
- cotangent: float32 [32, 128, 1536], P(('dp', 'fsdp')), may hold values from -6 to 6
- lengths: int32 [32], P(('dp', 'fsdp')), may hold values from 1 to 128, 2560 in all
- norm_gain: float32 [2, 1536], P('section'), may hold values from 0.5 to 1.5
- in_weight: bfloat16 [2, 1536, 6400], P('section', 'fsdp'), may hold values from -0.15625 to 0.15625
- dt_weight: bfloat16 [2, 1536, 48], P('section', 'fsdp'), may hold values from -0.15625 to 0.15625
- conv_weight: float32 [2, 4, 3328], P('section'), may hold values from -3 to 3
- conv_bias: float32 [2, 3328], P('section'), may hold values from -0.5 to 0.5
- dt_bias: float32 [2, 48], P('section'), may hold values from -4 to -1
- decay_log: float32 [2, 48], P('section'), may hold values from -4.6 to 0
- skip_gain: float32 [2, 48], P('section'), may hold values from 0.5 to 1.5
- gate_gain: float32 [2, 3072], P('section'), may hold values from 0.5 to 1.5
- out_weight: bfloat16 [2, 3072, 1536], P('section', 'fsdp'), may hold values from -0.109375 to 0.109375
Outputs:
- layer_outputs: float32 [2, 32, 128, 1536], P('section', ('dp', 'fsdp'))
- input_grads: float32 [2, 32, 128, 1536], P('section', ('dp', 'fsdp'))
- grad_norm_gain: float32 [2, 1536], P('section')
- grad_in_weight: float32 [2, 1536, 6400], P('section', 'fsdp')
- grad_dt_weight: float32 [2, 1536, 48], P('section', 'fsdp')
- grad_conv_weight: float32 [2, 4, 3328], P('section')
- grad_conv_bias: float32 [2, 3328], P('section')
- grad_dt_bias: float32 [2, 48], P('section')
- grad_decay_log: float32 [2, 48], P('section')
- grad_skip_gain: float32 [2, 48], P('section')
- grad_gate_gain: float32 [2, 3072], P('section')
- grad_out_weight: float32 [2, 3072, 1536], P('section', 'fsdp')
Inputs may be any that keep to these rules, and one draw needn't show every extreme that they name: `lengths`: positions from a sequence's length on are padding.
All inputs are finite; a program needn't handle non-finite values. No bound on the sum of `lengths` on one device may be relied on, other than what follows from the above.
Results may differ from a plain program's by a relative error of at most 0.011.
Values may be sent and summed in bfloat16 or wider, within the bound.
No kernel may reach another device: no remote copies, remote signals or barrier semaphores. Data moves between devices by JAX's collectives and lax.ppermute only.
A program may use at most 448 MiB of HBM per device.

v0:
```python
import jax
import jax.numpy as jnp
from jax import lax
from jax.sharding import PartitionSpec as P

INNER = 3072
HEADS = 48
HEAD_DIM = 64
STATE = 128
BLOCK = 64
CONV = 4
BUCKET = 128
MICRO = 2
epsilon = 1e-05
highest = lax.Precision.HIGHEST


def passed_along(block, axis, distance):
    devices = range(lax.axis_size(axis))
    route = [(i - distance, i) for i in devices if i - distance in devices]
    return lax.ppermute(block, axis, route)


def front_norm(residual, norm_gain):
    inverse = lax.rsqrt(jnp.mean(residual * residual, axis=-1, keepdims=True) + epsilon)
    return residual * inverse * norm_gain


def state_space(values, step_sizes, log_decay, inputs_b, outputs_c, skip_gain):
    seq_count, length = (values.shape[0], values.shape[1])
    blocks = length // BLOCK
    values_k = values.reshape(seq_count, blocks, BLOCK, HEADS, HEAD_DIM)
    steps_k = step_sizes.reshape(seq_count, blocks, BLOCK, HEADS)
    totals = jnp.cumsum(log_decay.reshape(seq_count, blocks, BLOCK, HEADS), axis=2)
    in_k = inputs_b.reshape(seq_count, blocks, BLOCK, STATE)
    out_k = outputs_c.reshape(seq_count, blocks, BLOCK, STATE)
    causal = (
        jnp.arange(BLOCK, dtype=jnp.int32)[:, None] >= jnp.arange(BLOCK, dtype=jnp.int32)[None, :]
    )[None, None, :, :, None]
    spread = totals[:, :, :, None, :] - totals[:, :, None, :, :]
    kernel = jnp.where(causal, jnp.exp(jnp.where(causal, spread, 0.0)), 0.0)
    inner_cb = jnp.einsum("skin,skjn->skij", out_k, in_k, precision=highest)
    weighted = inner_cb[..., None] * kernel * steps_k[:, :, None, :, :]
    local_part = jnp.einsum("skijh,skjhp->skihp", weighted, values_k, precision=highest)
    to_end = jnp.exp(totals[:, :, -1:, :] - totals) * steps_k
    scaled_values = values_k * to_end[..., None]
    block_states = jnp.einsum("skjhp,skjn->skhpn", scaled_values, in_k, precision=highest)
    carried = jnp.zeros((seq_count, HEADS, HEAD_DIM, STATE), jnp.float32)
    entering = []
    for block_index in range(blocks):
        entering.append(carried)
        carried = (
            jnp.exp(totals[:, block_index, -1, :])[:, :, None, None] * carried
            + block_states[:, block_index]
        )
    entering_all = jnp.stack(entering, axis=1)
    carried_part = (
        jnp.einsum("skin,skhpn->skihp", out_k, entering_all, precision=highest)
        * jnp.exp(totals)[..., None]
    )
    result = (local_part + carried_part).reshape(seq_count, length, HEADS, HEAD_DIM)
    return result + skip_gain[:, None] * values


def mixer_core(projected, dt_raw, conv_weight, conv_bias, dt_bias, decay_log, skip_gain, gate_gain):
    row_count = projected.shape[0]
    seq_count = row_count // BUCKET
    shaped = projected.reshape(seq_count, BUCKET, projected.shape[1])
    gate_part = shaped[:, :, :INNER]
    conv_input = shaped[:, :, INNER:]
    padded = jnp.pad(conv_input, ((0, 0), (CONV - 1, 0), (0, 0)))
    convolved = conv_bias + conv_weight[0] * padded[:, 0:BUCKET]
    for offset in range(1, CONV):
        convolved = convolved + conv_weight[offset] * padded[:, offset : offset + BUCKET]
    activated = jax.nn.silu(convolved)
    values = activated[:, :, :INNER].reshape(seq_count, BUCKET, HEADS, HEAD_DIM)
    inputs_b = activated[:, :, INNER : INNER + STATE]
    outputs_c = activated[:, :, INNER + STATE :]
    step_sizes = jax.nn.softplus(dt_raw.reshape(seq_count, BUCKET, HEADS) + dt_bias)
    log_decay = -jnp.exp(decay_log) * step_sizes
    scanned = state_space(values, step_sizes, log_decay, inputs_b, outputs_c, skip_gain).reshape(
        seq_count, BUCKET, INNER
    )
    gated_out = scanned * jax.nn.silu(gate_part)
    inverse = lax.rsqrt(jnp.mean(gated_out * gated_out, axis=-1, keepdims=True) + epsilon)
    return (gated_out * inverse * gate_gain).reshape(row_count, INNER)


def layer_forward(residual, params):
    norm_gain, in_weight, dt_weight, small_params, out_weight = params
    normed = front_norm(residual, norm_gain).astype(jnp.bfloat16)
    projected = jnp.dot(normed, in_weight, preferred_element_type=jnp.float32)
    dt_raw = jnp.dot(normed, dt_weight, preferred_element_type=jnp.float32)
    mixed_out = mixer_core(projected, dt_raw, *small_params).astype(jnp.bfloat16)
    output = residual + jnp.dot(mixed_out, out_weight, preferred_element_type=jnp.float32)
    return (output, (normed, projected, dt_raw, mixed_out))


def contract_rows(left, right):
    return lax.dot_general(
        left, right, (((0,), (0,)), ((), ())), preferred_element_type=jnp.float32
    )


def contract_cols(left, right):
    return lax.dot_general(
        left, right, (((1,), (1,)), ((), ())), preferred_element_type=jnp.float32
    )


def column_term(columns, grads):
    return contract_rows(columns, grads)


def reorder(columns, data_groups, owners):
    row_count, total_cols = columns.shape
    shaped = columns.reshape(row_count, owners, data_groups, total_cols // (owners * data_groups))
    return shaped.transpose(0, 2, 1, 3).reshape(row_count, total_cols)


def per_device(
    inputs,
    cotangent,
    lengths,
    norm_gain,
    in_weight,
    dt_weight,
    conv_weight,
    conv_bias,
    dt_bias,
    decay_log,
    skip_gain,
    gate_gain,
    out_weight,
):
    first_section = lax.axis_index("section") == 0
    full_in, full_dt, full_out = (
        lax.all_gather(in_weight[0], "fsdp", axis=0, tiled=True),
        lax.all_gather(dt_weight[0], "fsdp", axis=0, tiled=True),
        lax.all_gather(out_weight[0], "fsdp", axis=0, tiled=True),
    )
    small_params = (
        conv_weight[0],
        conv_bias[0],
        dt_bias[0],
        decay_log[0],
        skip_gain[0],
        gate_gain[0],
    )
    own_gain = norm_gain[0]
    params = (own_gain, full_in, full_dt, small_params, full_out)
    per_micro = inputs.shape[0] // MICRO
    row_count = per_micro * BUCKET
    model_width = inputs.shape[2]
    proj_cols = full_in.shape[1]
    data_groups = lax.axis_size("dp")
    owners = lax.axis_size("fsdp")
    positions = jnp.arange(BUCKET, dtype=jnp.int32)
    empty_rows = jnp.zeros((row_count, model_width), jnp.float32)

    def micro_rows(source, micro_index):
        return source[micro_index * per_micro : (micro_index + 1) * per_micro].reshape(
            row_count, model_width
        )

    def arrange(columns):
        return reorder(columns, data_groups, owners)

    layer_inputs = []
    results = []
    kept_all = []
    for section_tick in range(MICRO + 1):
        if section_tick > 0:
            arrived = passed_along(results[-1], "section", 1)
        else:
            arrived = empty_rows
        own_rows = micro_rows(inputs, section_tick) if section_tick < MICRO else empty_rows
        residual = jnp.where(first_section, own_rows, arrived)
        output, kept_values = layer_forward(residual, params)
        layer_inputs.append(residual)
        results.append(output)
        kept_all.append(kept_values)
    small_acc = (jnp.zeros(own_gain.shape, jnp.float32),) + tuple(
        (jnp.zeros(a.shape, jnp.float32) for a in small_params)
    )
    total_in = None
    total_out = None
    grads_back = []
    for section_tick in range(MICRO + 1):
        if section_tick > 0:
            returned = passed_along(grads_back[-1], "section", -1)
        else:
            returned = empty_rows
        if section_tick < MICRO:
            own_lengths = lengths[section_tick * per_micro : (section_tick + 1) * per_micro]
            live_rows = (positions[None, :] < own_lengths[:, None]).astype(jnp.float32)
            top_grad = micro_rows(cotangent, section_tick) * live_rows.reshape(row_count, 1)
        else:
            top_grad = empty_rows
        later_tick = min(section_tick + 1, MICRO)
        earlier = max(section_tick - 1, 0)
        grad_output = jnp.where(first_section, returned, top_grad)
        residual = jnp.where(first_section, layer_inputs[earlier], layer_inputs[later_tick])
        normed, projected, dt_raw, mixed_out = jax.tree.map(
            lambda a, b: jnp.where(first_section, a, b), kept_all[earlier], kept_all[later_tick]
        )
        grad_rounded = grad_output.astype(jnp.bfloat16)
        grad_mixed = contract_cols(grad_rounded, full_out)
        _, pull_mixer = jax.vjp(mixer_core, projected, dt_raw, *small_params)
        pulled = pull_mixer(grad_mixed)
        grad_proj = pulled[0].astype(jnp.bfloat16)
        grad_dt = pulled[1].astype(jnp.bfloat16)
        grad_cat = jnp.concatenate([grad_proj, grad_dt], axis=1)
        grad_normed = contract_cols(grad_proj, full_in) + contract_cols(grad_dt, full_dt)
        _, pull_front = jax.vjp(front_norm, residual, own_gain)
        grad_residual, grad_gain = pull_front(grad_normed)
        grads_back.append(grad_output + grad_residual)
        small_acc = tuple((a + b for a, b in zip(small_acc, (grad_gain,) + tuple(pulled[2:]))))
        normed_cols = arrange(normed)
        mixed_cols = arrange(mixed_out)
        part_in = lax.psum_scatter(
            column_term(normed_cols, grad_cat), ("dp", "fsdp"), scatter_dimension=0, tiled=True
        )
        part_out = lax.psum_scatter(
            column_term(mixed_cols, grad_rounded), ("dp", "fsdp"), scatter_dimension=0, tiled=True
        )
        total_in = part_in if total_in is None else total_in + part_in
        total_out = part_out if total_out is None else total_out + part_out
    owned_in, owned_out = (
        lax.all_gather(total_in, "dp", axis=0, tiled=True),
        lax.all_gather(total_out, "dp", axis=0, tiled=True),
    )
    small_total = lax.psum(small_acc, ("dp", "fsdp"))
    layer_out = jnp.concatenate(
        [
            jnp.where(first_section, results[m], results[m + 1]).reshape(
                per_micro, BUCKET, model_width
            )
            for m in range(MICRO)
        ],
        axis=0,
    )
    input_grad = jnp.concatenate(
        [
            jnp.where(first_section, grads_back[m + 1], grads_back[m]).reshape(
                per_micro, BUCKET, model_width
            )
            for m in range(MICRO)
        ],
        axis=0,
    )
    grad_in_part = owned_in[:, :proj_cols]
    grad_dt_part = owned_in[:, proj_cols:]
    return (
        layer_out[None],
        input_grad[None],
        small_total[0][None],
        grad_in_part[None],
        grad_dt_part[None],
        small_total[1][None],
        small_total[2][None],
        small_total[3][None],
        small_total[4][None],
        small_total[5][None],
        small_total[6][None],
        owned_out[None],
    )


def solution(mesh):
    in_specs = (
        P(("dp", "fsdp"), None, None),
        P(("dp", "fsdp"), None, None),
        P(("dp", "fsdp")),
        P("section", None),
        P("section", "fsdp", None),
        P("section", "fsdp", None),
        P("section", None, None),
        P("section", None),
        P("section", None),
        P("section", None),
        P("section", None),
        P("section", None),
        P("section", "fsdp", None),
    )
    out_specs = (
        P("section", ("dp", "fsdp"), None, None),
        P("section", ("dp", "fsdp"), None, None),
        P("section", None),
        P("section", "fsdp", None),
        P("section", "fsdp", None),
        P("section", None, None),
        P("section", None),
        P("section", None),
        P("section", None),
        P("section", None),
        P("section", None),
        P("section", "fsdp", None),
    )
    return jax.shard_map(
        per_device, mesh=mesh, in_specs=in_specs, out_specs=out_specs, check_vma=False
    )
```

profile of v0, /device:TPU:0, one launch (start us, length us, event | category | flops | bytes accessed | tf_op | source)
XLA Modules:
  0.0 1780.0 jit_solution(17367377292099813090)
XLA Ops:
  19.5 117.1 %all-gather.12.cloned.1.call-done = bf16[1,1536,6400]{2,1,0:T(8,128)(2,1)} async-done(((bf16[1,384,6400]{2,1,0:T(8,128)(2,1)}), bf16[1,1536,6400]{2,1,0:T(8,128)(2,1)}) %all-gather.12.cloned.1.call-update) | async-done | bytes 19660816 | tf_op jit(solution)/shard_map/all_gather | solution.py:138
  136.7 8.1 fusion.10
  184.4 18.1 %all-gather.14.cloned.1.call-done = bf16[1,3072,1536]{2,1,0:T(8,128)(2,1)} async-done(((bf16[1,768,1536]{2,1,0:T(8,128)(2,1)}), bf16[1,3072,1536]{2,1,0:T(8,128)(2,1)}) %all-gather.14.cloned.1.call-update) | async-done | bytes 9437200 | tf_op jit(solution)/shard_map/all_gather | solution.py:140
  214.1 14.1 collective-permute-done
  231.9 8.2 fusion.8
  310.2 8.7 fusion.396
  321.8 8.4 fusion.6
  388.8 9.2 fusion.241
  464.4 10.0 fusion.225
  571.6 14.4 fusion.4
  643.2 11.1 fusion.227
  681.2 8.2 fusion.344
  754.3 14.3 fusion.2
  792.6 21.3 %add_add_fusion.1 = f32[3072,1536]{1,0:T(8,128)} fusion(f32[3072,1536]{1,0:T(8,128)} %fusion.396, f32[3072,1536]{1,0:T(8,128)} %fusion.404, bf16[128,3072]{0,1:T(8,128)(2,1)} %bitcast.975, f32[128,1536]{1,0:T(8,128)} %collective-permute-done.3, pred[]{:T(512)S(6)} %eq.9), kind=kOutput, calls=%fused_computation.13 | convolution fusion | flops 1217593344 | bytes 58195968 | tf_op jit(solution)/shard_map/dot_general | solution.py:100
  834.1 19.9 %fusion.213 = f32[1536,6448]{1,0:T(8,128)} fusion(bf16[128,1536]{0,1:T(8,128)(2,1)S(1)} %bitcast.1029, bf16[128,48]{1,0:T(8,128)(2,1)} %bitcast.1059, bf16[128,6400]{1,0:T(8,128)(2,1)} %copy-done.45), kind=kOutput, calls=%fused_computation.278 | convolution fusion | flops 2538758144 | bytes 41660416 | tf_op jit(solution)/shard_map/dot_general | solution.py:100
  854.0 17.7 fusion.217
  921.3 10.7 fusion.229
  967.9 40.4 %add_add_fusion = f32[1536,6448]{1,0:T(8,128)} fusion(f32[1536,6448]{1,0:T(8,128)} %fusion.213, f32[1536,6448]{1,0:T(8,128)} %fusion.217, bf16[128,1536]{0,1:T(8,128)(2,1)S(1)} %bitcast.994, bf16[128,48]{1,0:T(8,128)(2,1)S(1)} %bitcast.1058, bf16[128,6400]{1,0:T(8,128)(2,1)S(1)} %fusion.232), kind=kOutput, calls=%fused_computation | convolution fusion | flops 2558566400 | bytes 120893440 | tf_op jit(solution)/shard_map/dot_general | solution.py:100
  1009.5 390.6 %reduce-scatter.3.cloned.1.call-done = f32[96,6448]{1,0:T(8,128)} async-done(((f32[1536,6448]{1,0:T(8,128)}), f32[96,6448]{1,0:T(8,128)}) %reduce-scatter.3.cloned.1.call-update) | async-done | bytes 2476048 | tf_op jit(solution)/shard_map/reduce_scatter | solution.py:221
  1414.6 10.4 fusion
  1433.2 56.9 %all-gather.10.cloned.1.call-done = f32[768,1536]{1,0:T(8,128)} async-done(((f32[192,1536]{1,0:T(8,128)}), f32[768,1536]{1,0:T(8,128)}) %all-gather.10.cloned.1.call-update) | async-done | bytes 4718608 | tf_op jit(solution)/shard_map/all_gather | solution.py:231
  1490.0 176.3 %all-gather.8.cloned.1.call-done = f32[384,6448]{1,0:T(8,128)} async-done(((f32[96,6448]{1,0:T(8,128)}), f32[384,6448]{1,0:T(8,128)}) %all-gather.8.cloned.1.call-update) | async-done | bytes 9904144 | tf_op jit(solution)/shard_map/all_gather | solution.py:230
  1666.3 8.3 slice_bitcast_fusion
  1676.3 83.1 %all-reduce.63.cloned.1.call-done = (f32[1,1536]{1,0:T(1,128)}, f32[1,4,3328]{2,1,0:T(4,128)}, f32[1,3328]{1,0:T(1,128)}, f32[1,48]{1,0:T(1,128)}, f32[1,48]{1,0...) async-done(((f32[1,1536]{1,0:T(1,128)}, f32[1,4,3328]{2,1,0:T(4,128)}, f32[1,3328]{1,0:T(1,128)}, f32[1,48]{1,0:T(1,128)}, f32[1,48]{1,0:T(1,128)}, ...) | async-done | bytes 85584 | tf_op jit(solution)/shard_map/psum | solution.py:233
  (949 shorter events, 676.6 us)
Async XLA Ops:
  7.2 129.5 %all-gather.12.cloned.1.call-start = ((), (), s32[]{:S(2)}) async-start(), calls=%async_computation.4 | async-start | bytes 24576000 | tf_op jit(solution)/shard_map/all_gather | solution.py:138
  8.0 194.5 %all-gather.14.cloned.1.call-start = ((), (), s32[]{:S(2)}) async-start(), calls=%async_computation.5 | async-start | bytes 11796480 | tf_op jit(solution)/shard_map/all_gather | solution.py:140
  8.7 1000.7 %reduce-scatter.5.cloned.1.call-start = ((), (), s32[]{:S(2)}) async-start(), calls=%async_computation.7 | async-start | bytes 20054016 | tf_op jit(solution)/shard_map/reduce_scatter | solution.py:224
  8.8 221.1 %copy-start.142 = (f32[1536]{0:T(1024)}, f32[1536]{0:T(1024)S(1)}, u32[]{:S(2)}) copy-start(f32[1536]{0:T(1024)S(1)} %reduce.80) | copy-start | bytes 18436
  8.9 137.6 %copy-start.211 = (f32[3328]{0:T(1024)}, f32[3328]{0:T(1024)S(1)}, u32[]{:S(2)}) copy-start(f32[3328]{0:T(1024)S(1)} %reduce.78) | copy-start | bytes 39940
  15.5 753.1 %copy-start.78 = (bf16[1,1536,48]{1,2,0:T(8,128)(2,1)}, bf16[1,1536,48]{1,2,0:T(8,128)(2,1)S(1)}, u32[]{:S(2)}) copy-start(bf16[1,1536,48]{1,2,0:T(8,128)(2,1)S(1)} %all-gather.1) | copy-start | bytes 442372
  15.7 129.1 %copy-start.261 = (f32[128]{0:T(128)}, f32[128]{0:T(128)S(1)}, u32[]{:S(2)}) copy-start(f32[128]{0:T(128)S(1)} %add_rsqrt_fusion.5) | copy-start | bytes 1540
  15.7 230.8 %copy-start.253 = (f32[48]{0:T(128)}, f32[48]{0:T(128)S(1)}, u32[]{:S(2)}) copy-start(f32[48]{0:T(128)S(1)} %bitcast_negate_fusion) | copy-start | bytes 580
  16.2 230.4 %copy-start.140 = (f32[128,48]{1,0:T(8,128)}, f32[128,48]{1,0:T(8,128)S(1)}, u32[]{:S(2)}) copy-start(f32[128,48]{1,0:T(8,128)S(1)} %get-tuple-element.253) | copy-start | bytes 73732
  19.3 268.4 %copy-start.135 = (f32[3072]{0:T(1024)}, f32[3072]{0:T(1024)S(1)}, u32[]{:S(2)}) copy-start(f32[3072]{0:T(1024)S(1)} %mul.1954) | copy-start | bytes 36868
  19.3 249.1 %copy-start.194 = (pred[64,64]{1,0:T(8,128)(4,1)}, pred[64,64]{1,0:T(8,128)(4,1)S(1)}, u32[]{:S(2)}) copy-start(pred[64,64]{1,0:T(8,128)(4,1)S(1)} %iota_compare_fusion) | copy-start | bytes 12292
  19.5 220.8 %copy-start.147 = (f32[3328]{0:T(1024)}, f32[3328]{0:T(1024)S(1)}, u32[]{:S(2)}) copy-start(f32[3328]{0:T(1024)S(1)} %get-tuple-element.111) | copy-start | bytes 39940
  19.5 220.8 %copy-start.152 = (f32[3328]{0:T(1024)}, f32[3328]{0:T(1024)S(1)}, u32[]{:S(2)}) copy-start(f32[3328]{0:T(1024)S(1)} %get-tuple-element.112) | copy-start | bytes 39940
  19.5 220.8 %copy-start.157 = (f32[3328]{0:T(1024)}, f32[3328]{0:T(1024)S(1)}, u32[]{:S(2)}) copy-start(f32[3328]{0:T(1024)S(1)} %get-tuple-element.113) | copy-start | bytes 39940
  19.5 220.8 %copy-start.162 = (f32[3328]{0:T(1024)}, f32[3328]{0:T(1024)S(1)}, u32[]{:S(2)}) copy-start(f32[3328]{0:T(1024)S(1)} %get-tuple-element.114) | copy-start | bytes 39940
  207.6 20.6 %collective-permute-start = (f32[128,1536]{1,0:T(8,128)S(1)}, f32[128,1536]{1,0:T(8,128)S(1)}, u32[]{:S(2)}, u32[]{:S(2)}) collective-permute-start(f32[128,1536]{1,0:T(8,128)S(1)} %fusion.150), channel_id=1, source_target_pairs={{0,16},{1,17},{2,18},{3,19},{4,20},{5,21},{6,22},{7,23},{8,24},{9,... | collective-permute-start | bytes 2359304 | tf_op jit(solution)/shard_map/ppermute | solution.py:21
  297.5 21.3 %collective-permute-start.1 = (f32[128,1536]{1,0:T(8,128)S(1)}, f32[128,1536]{1,0:T(8,128)S(1)}, u32[]{:S(2)}, u32[]{:S(2)}) collective-permute-start(f32[128,1536]{1,0:T(8,128)S(1)} %fusion.153), channel_id=1, source_target_pairs={{0,16},{1,17},{2,18},{3,19},{4,20},{5,21},{6,22},{7,23},{8,24},{9,... | collective-permute-start | bytes 2359304 | tf_op jit(solution)/shard_map/ppermute | solution.py:21
  589.5 20.9 %collective-permute-start.2 = (f32[128,1536]{1,0:T(8,128)}, f32[128,1536]{1,0:T(8,128)}, u32[]{:S(2)}, u32[]{:S(2)}) collective-permute-start(f32[128,1536]{1,0:T(8,128)} %fusion.374), channel_id=1, source_target_pairs={{16,0},{17,1},{18,2},{19,3},{20,4},{21,5},{22,6},{23,7},{24,8},{25... | collective-permute-start | bytes 2359304 | tf_op jit(solution)/shard_map/ppermute | solution.py:21
  772.7 19.9 %collective-permute-start.3 = (f32[128,1536]{1,0:T(8,128)}, f32[128,1536]{1,0:T(8,128)}, u32[]{:S(2)}, u32[]{:S(2)}) collective-permute-start(f32[128,1536]{1,0:T(8,128)} %get-tuple-element.146), channel_id=1, source_target_pairs={{16,0},{17,1},{18,2},{19,3},{20,4},{21,5},{22,6},{23,7},{24,8},{25... | collective-permute-start | bytes 2359304 | tf_op jit(solution)/shard_map/ppermute | solution.py:21
  813.9 586.2 %reduce-scatter.3.cloned.1.call-start = ((), (), s32[]{:S(2)}) async-start(), calls=%async_computation.6 | async-start | bytes 42614784 | tf_op jit(solution)/shard_map/reduce_scatter | solution.py:221
  1008.4 481.6 %all-gather.10.cloned.1.call-start = ((), (), s32[]{:S(2)}) async-start(), calls=%async_computation.3 | async-start | bytes 5898240 | tf_op jit(solution)/shard_map/all_gather | solution.py:231
  1009.4 390.9 %copy-start.81 = (f32[128,1536]{1,0:T(8,128)S(1)}, f32[128,1536]{1,0:T(8,128)}, u32[]{:S(2)}) copy-start(f32[128,1536]{1,0:T(8,128)} %copy-done.80) | copy-start | bytes 2359300
  1009.5 656.8 %all-gather.8.cloned.1.call-start = ((), (), s32[]{:S(2)}) async-start(), calls=%async_computation.2 | async-start | bytes 12533760 | tf_op jit(solution)/shard_map/all_gather | solution.py:230
  1400.2 359.1 %all-reduce.63.cloned.1.call-start = ((), (), s32[]{:S(2)}) async-start(), calls=%async_computation.8 | async-start | bytes 173056 | tf_op jit(solution)/shard_map/psum | solution.py:233
  (284 other events, 1908.2 us)
Sparse Core Ops, SparseCore 0:
  9.6 127.0 all-gather.11
  138.2 64.2 all-gather.13
  814.1 195.3 reduce-scatter.4
  1013.6 386.4 reduce-scatter.2
  1401.6 88.4 all-gather.9
  1491.4 174.7 all-gather.7
  1671.8 87.5 all-reduce.62
where the time goes:
time: 1790 us; the launch traced here: 1780 us
  waiting for transfers between devices  865 us (48%)
  matrix products  454 us (25%)
  local copies, waits for them, and re-layouts  295 us (16%)
  other arithmetic  132 us (7%)
    reduce_scatter x1, waiting for transfers between devices, per_device(): lax.psum_scatter(column_term(normed_cols, grad_cat), ('dp', 'fsdp'), scat...  391 us
    all_gather x1, waiting for transfers between devices, per_device(): lax.all_gather(total_in, 'dp', axis=0, tiled=True)  176 us
    all_gather x1, waiting for transfers between devices, per_device(): lax.all_gather(in_weight[0], 'fsdp', axis=0, tiled=True)  117 us
    dot_general x6, matrix products, contract_rows(): lax.dot_general(left, right, (((0,), (0,)), ((), ())), preferred_element_...  116 us
    dot_general x12, matrix products, state_space(): jnp.einsum('skijh,skjhp->skihp', weighted, values_k, precision=highest)  93.3 us
    psum x1, waiting for transfers between devices, per_device(): small_total = lax.psum(small_acc, ('dp', 'fsdp'))  83.1 us
    dot_general x9, matrix products, contract_cols(): lax.dot_general(left, right, (((1,), (1,)), ((), ())), preferred_element_...  67 us
    dot_general x12, matrix products, state_space(): jnp.einsum('skjhp,skjn->skhpn', scaled_values, in_k, precision=highest)  65.5 us
  transfers between devices with their start and end apart: 11, of which 10 were waited for; matrix products, arithmetic and copies ran while one was open for 18% of the time, Pallas kernels for 0%

commit v1 on v0

--- a/solution.py
+++ b/solution.py
@@ -133,6 +133,19 @@
     gate_gain,
     out_weight,
 ):
+
+    def _build_scenes(packet, d0):
+        seen = [packet]
+        world_n = jax.lax.axis_size("dp")
+        for num in range(1, world_n):
+            seen.append(
+                jax.lax.ppermute(
+                    seen[num - 1], "dp", [(j, (j - 1) % world_n) for j in range(world_n)]
+                )
+            )
+        right_arr = jnp.concatenate(seen, axis=d0)
+        return jnp.roll(right_arr, jax.lax.axis_index("dp") * packet.shape[d0], axis=d0)
+
     first_section = lax.axis_index("section") == 0
     full_in, full_dt, full_out = (
         lax.all_gather(in_weight[0], "fsdp", axis=0, tiled=True),
@@ -227,7 +240,7 @@
         total_in = part_in if total_in is None else total_in + part_in
         total_out = part_out if total_out is None else total_out + part_out
     owned_in, owned_out = (
-        lax.all_gather(total_in, "dp", axis=0, tiled=True),
+        _build_scenes(total_in, 0),
         lax.all_gather(total_out, "dp", axis=0, tiled=True),
     )
     small_total = lax.psum(small_acc, ("dp", "fsdp"))

time: 1790 us -> 1720 us (0.961)
  waiting for transfers between devices: 865 us -> 777 us
  local copies, waits for them, and re-layouts: 295 us -> 315 us
    ppermute x0 -> x3, waiting for transfers between devices: none -> 204 us  [_build_scenes(): jax.lax.ppermute(seen[num - 1], 'dp', [(j, (j - 1) % world_n) for j in ra...]
    all_gather x1 -> x0, waiting for transfers between devices: 176 us -> none  [per_device(): lax.all_gather(total_in, 'dp', axis=0, tiled=True)]
    all_gather x1, waiting for transfers between devices: 56.9 us -> 0.01 us  [per_device(): lax.all_gather(total_out, 'dp', axis=0, tiled=True)]
    psum x1, waiting for transfers between devices: 83.1 us -> 29.1 us  [per_device(): small_total = lax.psum(small_acc, ('dp', 'fsdp'))]
    unnamed x603 -> x610, local copies, waits for them, and re-layouts: 48.6 us -> 66.8 us
  transfers between devices with their start and end apart: 11 -> 13, of which waited for: 10 -> 11; matrix products, arithmetic and copies ran while one was open for 18% -> 20% of each run, Pallas kernels for 0% -> 0%
where the time goes in v1:
time: 1720 us
  waiting for transfers between devices  777 us (45%)
  matrix products  453 us (26%)
  local copies, waits for them, and re-layouts  315 us (18%)
  other arithmetic  132 us (8%)
  between operations  17.8 us (1%)
    reduce_scatter x1, waiting for transfers between devices, per_device(): lax.psum_scatter(column_term(normed_cols, grad_cat), ('dp', 'fsdp'), scat...  386 us
    ppermute x3, waiting for transfers between devices, _build_scenes(): jax.lax.ppermute(seen[num - 1], 'dp', [(j, (j - 1) % world_n) for j in ra...  204 us
    all_gather x1, waiting for transfers between devices, per_device(): lax.all_gather(in_weight[0], 'fsdp', axis=0, tiled=True)  117 us
    dot_general x6, matrix products, contract_rows(): lax.dot_general(left, right, (((0,), (0,)), ((), ())), preferred_element_...  116 us
    dot_general x12, matrix products, state_space(): jnp.einsum('skijh,skjhp->skihp', weighted, values_k, precision=highest)  93.2 us
    dot_general x9, matrix products, contract_cols(): lax.dot_general(left, right, (((1,), (1,)), ((), ())), preferred_element_...  67 us
    unnamed x610, local copies, waits for them, and re-layouts  66.8 us
    dot_general x12, matrix products, state_space(): jnp.einsum('skjhp,skjn->skhpn', scaled_values, in_k, precision=highest)  65.5 us
  transfers between devices with their start and end apart: 13, of which 11 were waited for; matrix products, arithmetic and copies ran while one was open for 20% of the time, Pallas kernels for 0%

profile of v1, /device:TPU:0, one launch (start us, length us, event | category | flops | bytes accessed | tf_op | source)
XLA Modules:
  0.0 1715.4 jit_solution(3765984533001470021)
XLA Ops:
  19.5 117.1 %all-gather.9.cloned.1.call-done = bf16[1,1536,6400]{2,1,0:T(8,128)(2,1)} async-done(((bf16[1,384,6400]{2,1,0:T(8,128)(2,1)}), bf16[1,1536,6400]{2,1,0:T(8,128)(2,1)}) %all-gather.9.cloned.1.call-update) | async-done | bytes 19660816 | tf_op jit(solution)/shard_map/all_gather | solution.py:151
  184.2 18.2 %all-gather.11.cloned.1.call-done = bf16[1,3072,1536]{2,1,0:T(8,128)(2,1)} async-done(((bf16[1,768,1536]{2,1,0:T(8,128)(2,1)}), bf16[1,3072,1536]{2,1,0:T(8,128)(2,1)}) %all-gather.11.cloned.1.call-update) | async-done | bytes 9437200 | tf_op jit(solution)/shard_map/all_gather | solution.py:153
  214.1 14.1 collective-permute-done
  231.9 8.2 fusion.8
  310.4 8.7 fusion.396
  322.0 8.4 fusion.6
  388.8 9.2 fusion.241
  464.4 10.0 fusion.225
  571.6 14.4 fusion.4
  643.3 11.2 fusion.227
  681.3 8.2 fusion.344
  754.4 14.3 fusion.2
  792.7 21.3 %add_add_fusion.1 = f32[3072,1536]{1,0:T(8,128)} fusion(f32[3072,1536]{1,0:T(8,128)} %fusion.396, f32[3072,1536]{1,0:T(8,128)} %fusion.404, bf16[128,3072]{0,1:T(8,128)(2,1)} %bitcast.975, f32[128,1536]{1,0:T(8,128)} %collective-permute-done.3, pred[]{:T(512)S(6)} %eq.12), kind=kOutput, calls=%fused_computation.13 | convolution fusion | flops 1217593344 | bytes 58195968 | tf_op jit(solution)/shard_map/dot_general | solution.py:100
  834.2 19.9 %fusion.213 = f32[1536,6448]{1,0:T(8,128)} fusion(bf16[128,1536]{0,1:T(8,128)(2,1)S(1)} %bitcast.1029, bf16[128,48]{1,0:T(8,128)(2,1)} %bitcast.1059, bf16[128,6400]{1,0:T(8,128)(2,1)} %copy-done.45), kind=kOutput, calls=%fused_computation.278 | convolution fusion | flops 2538758144 | bytes 41660416 | tf_op jit(solution)/shard_map/dot_general | solution.py:100
  854.2 17.7 %fusion.217 = f32[1536,6448]{1,0:T(8,128)} fusion(bf16[128,1536]{0,1:T(8,128)(2,1)} %bitcast.1030, bf16[128,48]{1,0:T(8,128)(2,1)S(1)} %bitcast.1060, bf16[128,6400]{1,0:T(8,128)(2,1)} %fusion.231), kind=kOutput, calls=%fused_computation.282 | convolution fusion | flops 2538758144 | bytes 41660416 | tf_op jit(solution)/shard_map/dot_general | solution.py:100
  921.4 10.7 fusion.229
  968.0 40.4 %add_add_fusion = f32[1536,6448]{1,0:T(8,128)} fusion(f32[1536,6448]{1,0:T(8,128)} %fusion.213, f32[1536,6448]{1,0:T(8,128)} %fusion.217, bf16[128,1536]{0,1:T(8,128)(2,1)S(1)} %bitcast.994, bf16[128,48]{1,0:T(8,128)(2,1)S(1)} %bitcast.1058, bf16[128,6400]{1,0:T(8,128)(2,1)S(1)} %fusion.232), kind=kOutput, calls=%fused_computation | convolution fusion | flops 2558566400 | bytes 120893440 | tf_op jit(solution)/shard_map/dot_general | solution.py:100
  1013.9 386.4 %reduce-scatter.3.cloned.1.call-done = f32[96,6448]{1,0:T(8,128)} async-done(((f32[1536,6448]{1,0:T(8,128)}), f32[96,6448]{1,0:T(8,128)}) %reduce-scatter.3.cloned.1.call-update) | async-done | bytes 2476048 | tf_op jit(solution)/shard_map/reduce_scatter | solution.py:234
  1411.3 10.4 fusion
  1422.3 110.3 %collective-permute-done.4 = f32[96,6448]{1,0:T(8,128)} collective-permute-done((f32[96,6448]{1,0:T(8,128)}, f32[96,6448]{1,0:T(8,128)}, u32[]{:S(2)}, u32[]{:S(2)}) %collective-permute-start.4) | collective-permute-done | bytes 2476064 | tf_op jit(solution)/shard_map/ppermute | solution.py:142
  1539.9 48.9 %collective-permute-done.5 = f32[96,6448]{1,0:T(8,128)} collective-permute-done((f32[96,6448]{1,0:T(8,128)}, f32[96,6448]{1,0:T(8,128)}, u32[]{:S(2)}, u32[]{:S(2)}) %collective-permute-start.5) | collective-permute-done | bytes 2476064 | tf_op jit(solution)/shard_map/ppermute | solution.py:142
  1599.1 44.6 %collective-permute-done.6 = f32[96,6448]{1,0:T(8,128)S(1)} collective-permute-done((f32[96,6448]{1,0:T(8,128)}, f32[96,6448]{1,0:T(8,128)S(1)}, u32[]{:S(2)}, u32[]{:S(2)}) %collective-permute-start.6) | collective-permute-done | bytes 2476064 | tf_op jit(solution)/shard_map/ppermute | solution.py:142
  1655.3 8.4 dynamic-slice_bitcast_fusion
  1665.6 29.1 %all-reduce.63.cloned.1.call-done = (f32[1,1536]{1,0:T(1,128)}, f32[1,4,3328]{2,1,0:T(4,128)}, f32[1,3328]{1,0:T(1,128)}, f32[1,48]{1,0:T(1,128)}, f32[1,48]{1,0...) async-done(((f32[1,1536]{1,0:T(1,128)}, f32[1,4,3328]{2,1,0:T(4,128)}, f32[1,3328]{1,0:T(1,128)}, f32[1,48]{1,0:T(1,128)}, f32[1,48]{1,0:T(1,128)}, ...) | async-done | bytes 85584 | tf_op jit(solution)/shard_map/psum | solution.py:246
  (960 shorter events, 707.2 us)
Async XLA Ops:
  7.2 129.5 %all-gather.9.cloned.1.call-start = ((), (), s32[]{:S(2)}) async-start(), calls=%async_computation.3 | async-start | bytes 24576000 | tf_op jit(solution)/shard_map/all_gather | solution.py:151
  8.0 194.5 %all-gather.11.cloned.1.call-start = ((), (), s32[]{:S(2)}) async-start(), calls=%async_computation.4 | async-start | bytes 11796480 | tf_op jit(solution)/shard_map/all_gather | solution.py:153
  8.7 1000.8 %reduce-scatter.5.cloned.1.call-start = ((), (), s32[]{:S(2)}) async-start(), calls=%async_computation.6 | async-start | bytes 20054016 | tf_op jit(solution)/shard_map/reduce_scatter | solution.py:237
  8.8 221.1 %copy-start.143 = (f32[1536]{0:T(1024)}, f32[1536]{0:T(1024)S(1)}, u32[]{:S(2)}) copy-start(f32[1536]{0:T(1024)S(1)} %reduce.80) | copy-start | bytes 18436
  15.5 753.2 %copy-start.79 = (bf16[1,1536,48]{1,2,0:T(8,128)(2,1)}, bf16[1,1536,48]{1,2,0:T(8,128)(2,1)S(1)}, u32[]{:S(2)}) copy-start(bf16[1,1536,48]{1,2,0:T(8,128)(2,1)S(1)} %all-gather.1) | copy-start | bytes 442372
  15.7 230.8 %copy-start.254 = (f32[48]{0:T(128)}, f32[48]{0:T(128)S(1)}, u32[]{:S(2)}) copy-start(f32[48]{0:T(128)S(1)} %bitcast_negate_fusion) | copy-start | bytes 580
  16.2 230.4 %copy-start.141 = (f32[128,48]{1,0:T(8,128)}, f32[128,48]{1,0:T(8,128)S(1)}, u32[]{:S(2)}) copy-start(f32[128,48]{1,0:T(8,128)S(1)} %get-tuple-element.253) | copy-start | bytes 73732
  19.3 268.7 %copy-start.136 = (f32[3072]{0:T(1024)}, f32[3072]{0:T(1024)S(1)}, u32[]{:S(2)}) copy-start(f32[3072]{0:T(1024)S(1)} %mul.1957) | copy-start | bytes 36868
  19.3 249.1 %copy-start.195 = (pred[64,64]{1,0:T(8,128)(4,1)}, pred[64,64]{1,0:T(8,128)(4,1)S(1)}, u32[]{:S(2)}) copy-start(pred[64,64]{1,0:T(8,128)(4,1)S(1)} %iota_compare_fusion) | copy-start | bytes 12292
  19.5 220.8 %copy-start.148 = (f32[3328]{0:T(1024)}, f32[3328]{0:T(1024)S(1)}, u32[]{:S(2)}) copy-start(f32[3328]{0:T(1024)S(1)} %get-tuple-element.111) | copy-start | bytes 39940
  19.5 220.8 %copy-start.153 = (f32[3328]{0:T(1024)}, f32[3328]{0:T(1024)S(1)}, u32[]{:S(2)}) copy-start(f32[3328]{0:T(1024)S(1)} %get-tuple-element.112) | copy-start | bytes 39940
  19.5 220.8 %copy-start.158 = (f32[3328]{0:T(1024)}, f32[3328]{0:T(1024)S(1)}, u32[]{:S(2)}) copy-start(f32[3328]{0:T(1024)S(1)} %get-tuple-element.113) | copy-start | bytes 39940
  19.5 220.8 %copy-start.163 = (f32[3328]{0:T(1024)}, f32[3328]{0:T(1024)S(1)}, u32[]{:S(2)}) copy-start(f32[3328]{0:T(1024)S(1)} %get-tuple-element.114) | copy-start | bytes 39940
  207.6 20.6 %collective-permute-start = (f32[128,1536]{1,0:T(8,128)S(1)}, f32[128,1536]{1,0:T(8,128)S(1)}, u32[]{:S(2)}, u32[]{:S(2)}) collective-permute-start(f32[128,1536]{1,0:T(8,128)S(1)} %fusion.150), channel_id=1, source_target_pairs={{0,16},{1,17},{2,18},{3,19},{4,20},{5,21},{6,22},{7,23},{8,24},{9,... | collective-permute-start | bytes 2359304 | tf_op jit(solution)/shard_map/ppermute | solution.py:21
  297.8 21.3 %collective-permute-start.1 = (f32[128,1536]{1,0:T(8,128)S(1)}, f32[128,1536]{1,0:T(8,128)S(1)}, u32[]{:S(2)}, u32[]{:S(2)}) collective-permute-start(f32[128,1536]{1,0:T(8,128)S(1)} %fusion.153), channel_id=1, source_target_pairs={{0,16},{1,17},{2,18},{3,19},{4,20},{5,21},{6,22},{7,23},{8,24},{9,... | collective-permute-start | bytes 2359304 | tf_op jit(solution)/shard_map/ppermute | solution.py:21
  589.6 20.9 %collective-permute-start.2 = (f32[128,1536]{1,0:T(8,128)}, f32[128,1536]{1,0:T(8,128)}, u32[]{:S(2)}, u32[]{:S(2)}) collective-permute-start(f32[128,1536]{1,0:T(8,128)} %fusion.374), channel_id=1, source_target_pairs={{16,0},{17,1},{18,2},{19,3},{20,4},{21,5},{22,6},{23,7},{24,8},{25... | collective-permute-start | bytes 2359304 | tf_op jit(solution)/shard_map/ppermute | solution.py:21
  772.8 19.9 %collective-permute-start.3 = (f32[128,1536]{1,0:T(8,128)}, f32[128,1536]{1,0:T(8,128)}, u32[]{:S(2)}, u32[]{:S(2)}) collective-permute-start(f32[128,1536]{1,0:T(8,128)} %get-tuple-element.146), channel_id=1, source_target_pairs={{16,0},{17,1},{18,2},{19,3},{20,4},{21,5},{22,6},{23,7},{24,8},{25... | collective-permute-start | bytes 2359304 | tf_op jit(solution)/shard_map/ppermute | solution.py:21
  814.0 586.3 %reduce-scatter.3.cloned.1.call-start = ((), (), s32[]{:S(2)}) async-start(), calls=%async_computation.5 | async-start | bytes 42614784 | tf_op jit(solution)/shard_map/reduce_scatter | solution.py:234
  1008.5 531.4 %all-gather.7.cloned.1.call-start = ((), (), s32[]{:S(2)}) async-start(), calls=%async_computation.2 | async-start | bytes 5898240 | tf_op jit(solution)/shard_map/all_gather | solution.py:244
  1009.5 392.1 %copy-start.77 = (bf16[1,128,3072]{2,1,0:T(8,128)(2,1)S(1)}, bf16[1,128,3072]{2,1,0:T(8,128)(2,1)}, u32[]{:S(2)}) copy-start(bf16[1,128,3072]{2,1,0:T(8,128)(2,1)} %get-tuple-element.123) | copy-start | bytes 2359300
  1009.6 685.1 %all-reduce.63.cloned.1.call-start = ((), (), s32[]{:S(2)}) async-start(), calls=%async_computation.7 | async-start | bytes 173056 | tf_op jit(solution)/shard_map/psum | solution.py:246
  1400.3 132.3 %collective-permute-start.4 = (f32[96,6448]{1,0:T(8,128)}, f32[96,6448]{1,0:T(8,128)}, u32[]{:S(2)}, u32[]{:S(2)}) collective-permute-start(f32[96,6448]{1,0:T(8,128)} %reduce-scatter.3.cloned.1.call-done), channel_id=1, source_target_pairs={{0,12},{4,0},{8,4},{12,8},{1,13},{5,1},{9,5},{13,9},{2,14},{6,2},{... | collective-permute-start | bytes 7428104 | tf_op jit(solution)/shard_map/ppermute | solution.py:142
  1532.6 56.2 %collective-permute-start.5 = (f32[96,6448]{1,0:T(8,128)}, f32[96,6448]{1,0:T(8,128)}, u32[]{:S(2)}, u32[]{:S(2)}) collective-permute-start(f32[96,6448]{1,0:T(8,128)} %collective-permute-done.4), channel_id=1, source_target_pairs={{0,12},{4,0},{8,4},{12,8},{1,13},{5,1},{9,5},{13,9},{2,14},{6,2},{... | collective-permute-start | bytes 7428104 | tf_op jit(solution)/shard_map/ppermute | solution.py:142
  1588.8 55.0 %collective-permute-start.6 = (f32[96,6448]{1,0:T(8,128)}, f32[96,6448]{1,0:T(8,128)S(1)}, u32[]{:S(2)}, u32[]{:S(2)}) collective-permute-start(f32[96,6448]{1,0:T(8,128)} %collective-permute-done.5), channel_id=1, source_target_pairs={{0,12},{4,0},{8,4},{12,8},{1,13},{5,1},{9,5},{13,9},{2,14},{6,2},{... | collective-permute-start | bytes 7428104 | tf_op jit(solution)/shard_map/ppermute | solution.py:142
  (286 other events, 4563.4 us)
Sparse Core Ops, SparseCore 0:
  9.6 127.0 all-gather.8
  138.2 64.2 all-gather.10
  814.2 195.3 reduce-scatter.4
  1013.7 386.5 reduce-scatter.2
  1401.7 130.1 all-gather.6
  1537.3 157.3 all-reduce.62
